TPU v7x, 256 devices: a whole 4x4x8 slice. The times are simulated.
256 devices in a mesh: dp: 64 (over x_lo, y, z), ep: 4 (over x_hi, core).
Axes of the slice: x: 4 (x_hi: 2, x_lo: 2; x = x_hi * 2 + x_lo), y: 4, z: 8, core: 2. Of those that a mesh axis runs over, the one named last changes fastest.
Arguments:
- tokens: bfloat16 [1024, 4096], P(('dp', 'ep')), may hold values from -6 to 6
- router: float32 [4096, 8], replicated, may hold values from -0.1875 to 0.1875
- expert_ids: int32 [1024, 2], P(('dp', 'ep')), may hold values from 0 to 7, all different within a row; in each aligned block of 4 rows (0 to 3, 4 to 7, ...) at most 2 rows name the same one
- w_gate: bfloat16 [64, 4096, 1536], P('dp', None, 'ep'), may hold values from -0.09375 to 0.09375
- w_up: bfloat16 [64, 4096, 1536], P('dp', None, 'ep'), may hold values from -0.09375 to 0.09375
- w_down: bfloat16 [64, 1536, 4096], P('dp', 'ep'), may hold values from -0.0546875 to 0.0546875
- states: bfloat16 [1024, 16, 8192], P('dp', None, 'ep'), may hold values from -6 to 6
- kv_blocks: bfloat16 [2048, 2, 16, 1024], P('dp', None, None, 'ep'), may hold values from -6 to 6
- plan_slots: int32 [64, 2, 3], replicated, may hold values from -1 to 63, as said below
- plan_len: int32 [64, 2], replicated, may hold values from 0 to 32, as said below
- plan_blocks: int32 [64, 2, 2, 2], replicated, may hold values from -1 to 31, as said below
Outputs:
- mixed: bfloat16 [1024, 4096], P(('dp', 'ep'))
- new_states: bfloat16 [1024, 16, 8192], P('dp', None, 'ep')
- new_cache: bfloat16 [2048, 2, 16, 1024], P('dp', None, None, 'ep')
Inputs may be any that keep to these rules, and one draw needn't show every extreme that they name: `expert_ids`: in the rows of one device no expert is named more than 2 times. `plan_slots`: A move is live exactly where its first entry is not -1, and then all three entries are set; otherwise all are -1. For each m there is one distance d_m from 1 to 63, distinct for distinct m, such that every live move (r, m) goes to rank (r + d_m) mod 64. The leaving slots of a rank are distinct, the slots taken at a rank are distinct and differ from its leaving slots. Some rank has all 2 moves live. `plan_len`: zero exactly where the move is not live; some move holds 32 tokens. `plan_blocks`: entry j of both tables is -1 exactly where j * 16 >= plan_len. The blocks leaving a rank are distinct, the blocks taken at a rank are distinct and differ from the ones leaving it.
All inputs are finite; a program needn't handle non-finite values.
Results may differ from a plain program's by a relative error of at most 0.005.
Values may be sent and summed in bfloat16 or wider, within the bound.
No kernel may reach another device: no remote copies, remote signals or barrier semaphores. Data moves between devices by JAX's collectives and lax.ppermute only.
A program may use at most 128 MiB of HBM per device.

v0:
```python
import jax
import jax.numpy as jnp
from jax import lax
from jax.sharding import PartitionSpec as P

CAP = 2


def passed_along(value, axis, steps):
    count = lax.axis_size(axis)
    pairs = [(source, (source + steps) % count) for source in range(count)]
    return lax.ppermute(value, axis, pairs)


def hop_along(item_pair, distance, ranks):
    steps_needed = (ranks - 1).bit_length()
    for level in range(steps_needed):
        moved = passed_along((item_pair[0], item_pair[1]), "dp", 1 << level)
        taken = distance >> level & 1 == 1
        item_pair = (
            jnp.where(taken, moved[0], item_pair[0]),
            jnp.where(taken, moved[1], item_pair[1]),
        )
    return item_pair


def local(
    tokens,
    router,
    expert_ids,
    w_gate,
    w_up,
    w_down,
    states,
    kv_blocks,
    plan_slots,
    plan_len,
    plan_blocks,
):
    ranks = lax.axis_size("dp")
    here = lax.axis_index("dp")
    moves = plan_slots.shape[1]
    slot_count = states.shape[0]
    block_count = kv_blocks.shape[0]
    per_request = plan_blocks.shape[3]
    block_len = kv_blocks.shape[2]
    mine = lax.dynamic_index_in_dim(plan_slots, here, 0, keepdims=False)
    my_blocks = lax.dynamic_index_in_dim(plan_blocks, here, 0, keepdims=False)
    my_length = lax.dynamic_index_in_dim(plan_len, here, 0, keepdims=False)
    leaving_slot = mine[:, 0]
    leaving_block = my_blocks[:, 0, :]
    state_out = states[jnp.maximum(leaving_slot, 0)]
    state_out = jnp.where((leaving_slot >= 0)[:, None, None], state_out, jnp.zeros_like(state_out))
    cache_out = kv_blocks[jnp.maximum(leaving_block, 0)]
    position = jnp.arange(per_request)[:, None] * block_len + jnp.arange(block_len)[None, :]
    written = (leaving_block >= 0)[:, :, None] & (position[None] < my_length[:, None, None])
    cache_out = jnp.where(written[:, :, None, :, None], cache_out, jnp.zeros_like(cache_out))
    arrivals = plan_slots[:, :, 1] == here
    sender = jnp.sum(jnp.where(arrivals, jnp.arange(ranks)[:, None], 0), axis=0)
    arriving = jnp.any(arrivals, axis=0)
    rank_line = jnp.arange(ranks, dtype=jnp.int32)
    live_all = plan_slots[:, :, 0] >= 0
    span = jnp.where(live_all, (plan_slots[:, :, 1] - rank_line[:, None]) % ranks, 0)
    distance_of = jnp.max(span, axis=0)
    state_list = []
    cache_list = []
    for move_index in range(moves):
        got = hop_along(
            (state_out[move_index], cache_out[move_index]), distance_of[move_index], ranks
        )
        state_list.append(got[0])
        cache_list.append(got[1])
    state_in = jnp.stack(state_list, axis=0)
    cache_in = jnp.stack(cache_list, axis=0)
    slot_line = jnp.arange(slot_count)
    gone = jnp.any(slot_line[:, None] == leaving_slot[None, :], axis=1)
    new_states = jnp.where(gone[:, None, None], jnp.zeros_like(states), states)
    block_line = jnp.arange(block_count)
    gone_blocks = jnp.any(block_line[:, None, None] == leaving_block[None], axis=(1, 2))
    new_cache = jnp.where(gone_blocks[:, None, None, None], jnp.zeros_like(kv_blocks), kv_blocks)
    for move_index in range(moves):
        anchor = sender[move_index]
        place = plan_slots[anchor, move_index, 2]
        landing = (slot_line == place) & arriving[move_index]
        new_states = jnp.where(landing[:, None, None], state_in[move_index][None], new_states)
        for block_index in range(per_request):
            spot = plan_blocks[anchor, move_index, 1, block_index]
            block_hit = (block_line == spot) & arriving[move_index]
            new_cache = jnp.where(
                block_hit[:, None, None, None], cache_in[move_index, block_index][None], new_cache
            )
    experts = router.shape[1]
    tok_count = tokens.shape[0]
    width = tokens.shape[1]
    group = ranks // experts
    flat_ids = expert_ids.reshape(-1)
    onehot = (flat_ids[:, None] == jnp.arange(experts)[None, :]).astype(jnp.int32)
    earlier = jnp.cumsum(onehot, axis=0) - onehot
    slot_of = jnp.sum(earlier * onehot, axis=1)
    target_row = flat_ids * CAP + slot_of
    placer = (jnp.arange(experts * CAP)[:, None] == target_row[None, :]).astype(jnp.bfloat16)
    doubled = jnp.repeat(tokens, 2, axis=0)
    packed = jnp.dot(placer, doubled, preferred_element_type=jnp.float32).astype(jnp.bfloat16)
    outgoing = jnp.repeat(packed.reshape(experts, CAP, width), group, axis=0)
    incoming = lax.all_to_all(outgoing, "dp", split_axis=0, concat_axis=0, tiled=True)
    rows_in = incoming.reshape(ranks * CAP, width)
    piece = lax.all_gather(rows_in, "ep", axis=0, tiled=True)
    gate = jnp.dot(piece, w_gate[0], preferred_element_type=jnp.float32)
    upper = jnp.dot(piece, w_up[0], preferred_element_type=jnp.float32)
    hidden = (jax.nn.silu(gate) * upper).astype(jnp.bfloat16)
    summed = lax.psum_scatter(
        jnp.dot(hidden, w_down[0], preferred_element_type=jnp.float32),
        "ep",
        scatter_dimension=0,
        tiled=True,
    )
    returned = lax.all_to_all(
        summed.reshape(ranks, CAP, width), "dp", split_axis=0, concat_axis=0, tiled=True
    )
    expert_out = jnp.sum(returned.reshape(experts, group, CAP, width), axis=1).reshape(
        experts * CAP, width
    )
    chosen = expert_out[target_row].reshape(tok_count, 2, width)
    logits = jnp.dot(tokens.astype(jnp.float32), router, precision=lax.Precision.HIGHEST)
    scores = jax.nn.sigmoid(jnp.take_along_axis(logits, expert_ids, axis=1))
    weights = scores / jnp.sum(scores, axis=1, keepdims=True)
    mixed = jnp.sum(weights[:, :, None] * chosen, axis=1).astype(jnp.bfloat16)
    return (mixed, new_states, new_cache)


def solution(mesh):
    placed = (
        P(("dp", "ep"), None),
        P(),
        P(("dp", "ep"), None),
        P("dp", None, "ep"),
        P("dp", None, "ep"),
        P("dp", "ep", None),
        P("dp", None, "ep"),
        P("dp", None, None, "ep"),
        P(),
        P(),
        P(),
    )
    return jax.shard_map(
        local,
        mesh=mesh,
        in_specs=placed,
        out_specs=(P(("dp", "ep"), None), P("dp", None, "ep"), P("dp", None, None, "ep")),
        check_vma=False,
    )
```

profile of v0, /device:TPU:34, one launch (start us, length us, event | category | flops | bytes accessed | tf_op | source)
XLA Modules:
  0.0 283.0 jit_solution(17758954699944343621)
XLA Ops:
  7.2 0.9 broadcast_in_dim.175
  8.2 0.8 copy.30
  9.4 0.5 copy-done.6
  10.1 1.0 broadcast_in_dim.176
  11.1 42.1 %all_to_all.10 = bf16[64,2,4096]{2,1,0:T(2,128)(2,1)} all-to-all(bf16[64,2,4096]{2,1,0:T(2,128)(2,1)S(1)} %bitcast.101), channel_id=1, replica_groups=mesh['dp'=64,'ep'=4] {'dp'}, dimensions={0} | all-to-all | bytes 2097152 | tf_op jit(solution)/shard_map/all_to_all | solution.py:105
  53.2 2.2 reshape.263
  55.6 36.1 %all-gather.2.cloned.1.call-done = bf16[512,4096]{1,0:T(8,128)(2,1)} async-done(((bf16[128,4096]{1,0:T(8,128)(2,1)}), bf16[512,4096]{1,0:T(8,128)(2,1)}) %all-gather.2.cloned.1.call-update) | async-done | bytes 4194320 | tf_op jit(solution)/shard_map/all_gather | solution.py:107
  91.7 6.4 %fusion.4 = f32[512,384]{1,0:T(8,128)} fusion(bf16[512,4096]{1,0:T(8,128)(2,1)} %all-gather.2.cloned.1.call-done, bf16[1,4096,384]{2,1,0:T(8,128)(2,1)} %param.14), kind=kOutput, calls=%fused_computation.9 | convolution fusion | flops 1610612736 | bytes 8126464 | tf_op jit(solution)/shard_map/dot_general | solution.py:108
  98.1 11.0 %fusion = f32[512,4096]{1,0:T(8,128)} fusion(bf16[1,384,4096]{2,1,0:T(8,128)(2,1)S(1)} %copy-done, bf16[512,4096]{1,0:T(8,128)(2,1)} %all-gather.2.cloned.1.call-done, bf16[1,4096,384]{2,1,0:T(8,128)(2,1)} %param.15, f32[512,384]{1,0:T(8,128)} %fusion.4), kind=kOutput, calls=%fused_computation.5 | convolution fusion | flops 3222405120 | bytes 19660800 | tf_op jit(solution)/shard_map/dot_general | solution.py:112
  109.1 0.6 copy-done.3
  110.1 1.8 gather_fusion.1
  112.0 0.7 slice_bitcast_fusion.1
  112.7 1.6 collective-permute-start
  114.2 1.6 collective-permute-start.6
  116.1 0.9 fusion.22
  117.0 1.6 gather_fusion.2
  118.8 0.6 slice_bitcast_fusion.3
  119.5 2.8 collective-permute-start.12
  122.2 0.7 collective-permute-start.18
  123.0 0.6 fusion.29
  126.7 1.0 fusion.31
  127.7 0.7 gather_fusion.3
  129.8 0.6 constant_dynamic-slice_fusion.7
  130.4 0.7 constant_dynamic-slice_fusion.6
  131.2 0.7 fusion.30
  131.8 1.7 compare_and_fusion.1
  133.6 2.5 compare_and_fusion.5
  136.1 0.6 fusion.25
  136.7 0.6 fusion.28
  137.4 0.7 compare_reduce_fusion.1
  138.1 0.8 compare_reduce_fusion
  138.9 2.0 compare_and_fusion.3
  147.9 0.8 collective-permute-start.19
  148.8 1.8 collective-permute-start.13
  150.6 0.9 broadcast_select_fusion.8
  151.5 2.6 collective-permute-start.7
  154.1 2.8 %collective-permute-start.1 = (bf16[16,2048]{1,0:T(8,128)(2,1)S(1)}, bf16[16,2048]{1,0:T(8,128)(2,1)S(1)}, u32[]{:S(2)}, u32[]{:S(2)}) collective-permute-start(bf16[16,2048]{1,0:T(8,128)(2,1)S(1)} %get-tuple-element.7), channel_id=1, source_target_pairs={{0,8},{4,12},{8,16},{12,20},{16,24},{20,28},{24,32},{28,36},{32,40... | collective-permute-start | bytes 196616 | tf_op jit(solution)/shard_map/ppermute | solution.py:12
  157.2 1.9 collective-permute-start.20
  159.1 4.9 %collective-permute-start.14 = (bf16[2,2,16,256]{3,2,1,0:T(8,128)(2,1)S(1)}, bf16[2,2,16,256]{3,2,1,0:T(8,128)(2,1)S(1)}, u32[]{:S(2)}, u32[]{:S(2)}) collective-permute-start(bf16[2,2,16,256]{3,2,1,0:T(8,128)(2,1)S(1)} %broadcast_select_fusion.20), channel_id=1, source_target_pairs={{0,16},{4,20},{8,24},{12,28},{16,32},{20,36},{24,40},{28,44},{32,4... | collective-permute-start | bytes 98312 | tf_op jit(solution)/shard_map/ppermute | solution.py:12
  164.0 4.5 %collective-permute-done.20 = bf16[2,2,16,256]{3,2,1,0:T(8,128)(2,1)S(1)} collective-permute-done((bf16[2,2,16,256]{3,2,1,0:T(8,128)(2,1)S(1)}, bf16[2,2,16,256]{3,2,1,0:T(8,128)(2,1)S(1)}, u32[]{:S(2)}, u32[]{:S(2)}) %collective-permute-start.20) | collective-permute-done | bytes 32800 | tf_op jit(solution)/shard_map/ppermute | solution.py:12
  168.6 1.5 collective-permute-done.14
  170.2 3.3 %collective-permute-start.8 = (bf16[16,2048]{1,0:T(8,128)(2,1)S(1)}, bf16[16,2048]{1,0:T(8,128)(2,1)S(1)}, u32[]{:S(2)}, u32[]{:S(2)}) collective-permute-start(bf16[16,2048]{1,0:T(8,128)(2,1)S(1)} %broadcast_select_fusion.3), channel_id=1, source_target_pairs={{0,16},{4,20},{8,24},{12,28},{16,32},{20,36},{24,40},{28,44},{32,4... | collective-permute-start | bytes 196616 | tf_op jit(solution)/shard_map/ppermute | solution.py:12
  173.6 2.6 collective-permute-start.2
  176.1 5.7 %collective-permute-start.22 = (bf16[2,2,16,256]{3,2,1,0:T(8,128)(2,1)S(1)}, bf16[2,2,16,256]{3,2,1,0:T(8,128)(2,1)S(1)}, u32[]{:S(2)}, u32[]{:S(2)}) collective-permute-start(bf16[2,2,16,256]{3,2,1,0:T(8,128)(2,1)S(1)} %broadcast_select_fusion.17), channel_id=1, source_target_pairs={{0,64},{4,68},{8,72},{12,76},{16,80},{20,84},{24,88},{28,92},{32,9... | collective-permute-start | bytes 98312 | tf_op jit(solution)/shard_map/ppermute | solution.py:12
  182.0 2.0 collective-permute-done.22
  184.0 2.3 collective-permute-start.23
  186.3 2.6 collective-permute-done.16
  189.2 0.5 collective-permute-start.9
  189.8 3.7 %reduce-scatter.2.cloned.1.call-done = f32[128,4096]{1,0:T(8,128)} async-done(((f32[512,4096]{1,0:T(8,128)}), f32[128,4096]{1,0:T(8,128)}) %reduce-scatter.2.cloned.1.call-update) | async-done | bytes 2097168 | tf_op jit(solution)/shard_map/reduce_scatter | solution.py:111
  193.5 3.5 %reshape.264 = f32[64,2,4096]{2,1,0:T(2,128)} reshape(f32[128,4096]{1,0:T(8,128)} %reduce-scatter.2.cloned.1.call-done) | data formatting | bytes 4194304 | tf_op jit(solution)/shard_map/reshape | solution.py:118
  197.0 21.6 %all-to-all-start.1 = ((f32[64,2,4096]{2,1,0:T(2,128)}), f32[64,2,4096]{2,1,0:T(2,128)}, u32[]{:S(2)}, u32[]{:S(2)}) async-start(f32[64,2,4096]{2,1,0:T(2,128)} %reshape.264), calls=%async_computation.2 | async-start | bytes 4194304 | tf_op jit(solution)/shard_map/all_to_all | solution.py:117
  218.7 2.2 select_select_fusion.1
  220.9 3.2 %collective-permute-start.10 = (bf16[16,2048]{1,0:T(8,128)(2,1)S(1)}, bf16[16,2048]{1,0:T(8,128)(2,1)S(1)}, u32[]{:S(2)}, u32[]{:S(2)}) collective-permute-start(bf16[16,2048]{1,0:T(8,128)(2,1)S(1)} %broadcast_select_fusion.5), channel_id=1, source_target_pairs={{0,64},{4,68},{8,72},{12,76},{16,80},{20,84},{24,88},{28,92},{32,9... | collective-permute-start | bytes 196616 | tf_op jit(solution)/shard_map/ppermute | solution.py:12
  224.0 0.4 collective-permute-start.4
  224.5 3.5 %collective-permute-done.10 = bf16[16,2048]{1,0:T(8,128)(2,1)S(1)} collective-permute-done((bf16[16,2048]{1,0:T(8,128)(2,1)S(1)}, bf16[16,2048]{1,0:T(8,128)(2,1)S(1)}, u32[]{:S(2)}, u32[]{:S(2)}) %collective-permute-start.10) | collective-permute-done | bytes 65568 | tf_op jit(solution)/shard_map/ppermute | solution.py:12
  228.0 2.0 collective-permute-start.11
  230.0 3.7 %collective-permute-done.4 = bf16[16,2048]{1,0:T(8,128)(2,1)S(1)} collective-permute-done((bf16[16,2048]{1,0:T(8,128)(2,1)S(1)}, bf16[16,2048]{1,0:T(8,128)(2,1)S(1)}, u32[]{:S(2)}, u32[]{:S(2)}) %collective-permute-start.4) | collective-permute-done | bytes 65568 | tf_op jit(solution)/shard_map/ppermute | solution.py:12
  233.8 4.5 %collective-permute-done.5 = bf16[16,2048]{1,0:T(8,128)(2,1)S(1)} collective-permute-done((bf16[16,2048]{1,0:T(8,128)(2,1)S(1)}, bf16[16,2048]{1,0:T(8,128)(2,1)S(1)}, u32[]{:S(2)}, u32[]{:S(2)}) %collective-permute-start.5) | collective-permute-done | bytes 65568 | tf_op jit(solution)/shard_map/ppermute | solution.py:12
  238.3 1.3 select_select_fusion
  239.6 30.9 %all-to-all-done.1 = f32[64,2,4096]{2,1,0:T(2,128)} async-done(((f32[64,2,4096]{2,1,0:T(2,128)}), f32[64,2,4096]{2,1,0:T(2,128)}, u32[]{:S(2)}, u32[]{:S(2)}) %all-to-all-start.1) | async-done | bytes 2097184 | tf_op jit(solution)/shard_map/all_to_all | solution.py:117
  270.5 3.0 %bitcast_reduce_fusion = f32[8,2,4096]{2,1,0:T(2,128)} fusion(f32[64,2,4096]{2,1,0:T(2,128)} %all-to-all-done.1), kind=kLoop, calls=%fused_computation.11 | loop fusion | flops 458752 | bytes 2359296 | tf_op jit(solution)/shard_map/reduce_sum | solution.py:120
  273.5 1.1 reshape.266
  274.6 0.6 gather_fusion
  275.3 0.9 multiply_reduce_fusion
  (100 shorter events, 3.9 us)
Async XLA Ops:
  7.2 90.9 %copy-start = (bf16[1,384,4096]{2,1,0:T(8,128)(2,1)S(1)}, bf16[1,384,4096]{2,1,0:T(8,128)(2,1)}, u32[]{:S(2)}) copy-start(bf16[1,384,4096]{2,1,0:T(8,128)(2,1)} %param.16) | copy-start | bytes 9437188
  7.2 84.5 %all-gather.2.cloned.1.call-start = ((), (), s32[]{:S(2)}) async-start(), calls=%async_computation.3 | async-start | bytes 5242880 | tf_op jit(solution)/shard_map/all_gather | solution.py:107
  9.4 0.5 copy-start.6
  55.5 138.0 %reduce-scatter.2.cloned.1.call-start = ((), (), s32[]{:S(2)}) async-start(), calls=%async_computation.4 | async-start | bytes 10485760 | tf_op jit(solution)/shard_map/reduce_scatter | solution.py:111
  109.1 0.7 copy-start.3
  109.1 6.7 %copy-start.4 = (s32[64,2,2,2]{0,3,2,1:T(2,128)S(1)}, s32[64,2,2,2]{0,3,2,1:T(2,128)}, u32[]{:S(2)}) copy-start(s32[64,2,2,2]{0,3,2,1:T(2,128)} %param.21) | copy-start | bytes 6148
  109.1 17.6 %copy-start.2 = (f32[4096,8]{0,1:T(8,128)S(1)}, f32[4096,8]{0,1:T(8,128)}, u32[]{:S(2)}) copy-start(f32[4096,8]{0,1:T(8,128)} %param.12) | copy-start | bytes 393220
  110.1 1.8 copy-start.7
  112.7 37.9 %collective-permute-start = (bf16[16,2048]{1,0:T(8,128)(2,1)}, bf16[16,2048]{1,0:T(8,128)(2,1)}, u32[]{:S(2)}, u32[]{:S(2)}) collective-permute-start(bf16[16,2048]{1,0:T(8,128)(2,1)} %get-tuple-element.9), channel_id=1, source_target_pairs={{0,4},{4,8},{8,12},{12,16},{16,20},{20,24},{24,28},{28,32},{32,36}... | collective-permute-start | bytes 196616 | tf_op jit(solution)/shard_map/ppermute | solution.py:12
  114.2 36.4 %collective-permute-start.6 = (bf16[16,2048]{1,0:T(8,128)(2,1)}, bf16[16,2048]{1,0:T(8,128)(2,1)}, u32[]{:S(2)}, u32[]{:S(2)}) collective-permute-start(bf16[16,2048]{1,0:T(8,128)(2,1)} %get-tuple-element.10), channel_id=1, source_target_pairs={{0,4},{4,8},{8,12},{12,16},{16,20},{20,24},{24,28},{28,32},{32,36}... | collective-permute-start | bytes 196616 | tf_op jit(solution)/shard_map/ppermute | solution.py:12
  116.0 2.7 copy-start.5
  119.5 28.4 %collective-permute-start.12 = (bf16[2,2,16,256]{3,2,1,0:T(8,128)(2,1)}, bf16[2,2,16,256]{3,2,1,0:T(8,128)(2,1)S(1)}, u32[]{:S(2)}, u32[]{:S(2)}) collective-permute-start(bf16[2,2,16,256]{3,2,1,0:T(8,128)(2,1)} %get-tuple-element.13), channel_id=1, source_target_pairs={{0,4},{4,8},{8,12},{12,16},{16,20},{20,24},{24,28},{28,32},{32,36}... | collective-permute-start | bytes 98312 | tf_op jit(solution)/shard_map/ppermute | solution.py:12
  122.2 25.7 %collective-permute-start.18 = (bf16[2,2,16,256]{3,2,1,0:T(8,128)(2,1)}, bf16[2,2,16,256]{3,2,1,0:T(8,128)(2,1)}, u32[]{:S(2)}, u32[]{:S(2)}) collective-permute-start(bf16[2,2,16,256]{3,2,1,0:T(8,128)(2,1)} %get-tuple-element.14), channel_id=1, source_target_pairs={{0,4},{4,8},{8,12},{12,16},{16,20},{20,24},{24,28},{28,32},{32,36}... | collective-permute-start | bytes 98312 | tf_op jit(solution)/shard_map/ppermute | solution.py:12
  147.9 9.2 %collective-permute-start.19 = (bf16[2,2,16,256]{3,2,1,0:T(8,128)(2,1)S(1)}, bf16[2,2,16,256]{3,2,1,0:T(8,128)(2,1)S(1)}, u32[]{:S(2)}, u32[]{:S(2)}) collective-permute-start(bf16[2,2,16,256]{3,2,1,0:T(8,128)(2,1)S(1)} %get-tuple-element.12), channel_id=1, source_target_pairs={{0,8},{4,12},{8,16},{12,20},{16,24},{20,28},{24,32},{28,36},{32,40... | collective-permute-start | bytes 98312 | tf_op jit(solution)/shard_map/ppermute | solution.py:12
  148.8 10.3 %collective-permute-start.13 = (bf16[2,2,16,256]{3,2,1,0:T(8,128)(2,1)S(1)}, bf16[2,2,16,256]{3,2,1,0:T(8,128)(2,1)S(1)}, u32[]{:S(2)}, u32[]{:S(2)}) collective-permute-start(bf16[2,2,16,256]{3,2,1,0:T(8,128)(2,1)S(1)} %get-tuple-element.11), channel_id=1, source_target_pairs={{0,8},{4,12},{8,16},{12,20},{16,24},{20,28},{24,32},{28,36},{32,40... | collective-permute-start | bytes 98312 | tf_op jit(solution)/shard_map/ppermute | solution.py:12
  151.5 18.7 %collective-permute-start.7 = (bf16[16,2048]{1,0:T(8,128)(2,1)S(1)}, bf16[16,2048]{1,0:T(8,128)(2,1)S(1)}, u32[]{:S(2)}, u32[]{:S(2)}) collective-permute-start(bf16[16,2048]{1,0:T(8,128)(2,1)S(1)} %get-tuple-element.8), channel_id=1, source_target_pairs={{0,8},{4,12},{8,16},{12,20},{16,24},{20,28},{24,32},{28,36},{32,40... | collective-permute-start | bytes 196616 | tf_op jit(solution)/shard_map/ppermute | solution.py:12
  154.1 19.4 %collective-permute-start.1 = (bf16[16,2048]{1,0:T(8,128)(2,1)S(1)}, bf16[16,2048]{1,0:T(8,128)(2,1)S(1)}, u32[]{:S(2)}, u32[]{:S(2)}) collective-permute-start(bf16[16,2048]{1,0:T(8,128)(2,1)S(1)} %get-tuple-element.7), channel_id=1, source_target_pairs={{0,8},{4,12},{8,16},{12,20},{16,24},{20,28},{24,32},{28,36},{32,40... | collective-permute-start | bytes 196616 | tf_op jit(solution)/shard_map/ppermute | solution.py:12
  157.2 11.4 %collective-permute-start.20 = (bf16[2,2,16,256]{3,2,1,0:T(8,128)(2,1)S(1)}, bf16[2,2,16,256]{3,2,1,0:T(8,128)(2,1)S(1)}, u32[]{:S(2)}, u32[]{:S(2)}) collective-permute-start(bf16[2,2,16,256]{3,2,1,0:T(8,128)(2,1)S(1)} %broadcast_select_fusion.15), channel_id=1, source_target_pairs={{0,16},{4,20},{8,24},{12,28},{16,32},{20,36},{24,40},{28,44},{32,4... | collective-permute-start | bytes 98312 | tf_op jit(solution)/shard_map/ppermute | solution.py:12
  159.1 11.0 %collective-permute-start.14 = (bf16[2,2,16,256]{3,2,1,0:T(8,128)(2,1)S(1)}, bf16[2,2,16,256]{3,2,1,0:T(8,128)(2,1)S(1)}, u32[]{:S(2)}, u32[]{:S(2)}) collective-permute-start(bf16[2,2,16,256]{3,2,1,0:T(8,128)(2,1)S(1)} %broadcast_select_fusion.20), channel_id=1, source_target_pairs={{0,16},{4,20},{8,24},{12,28},{16,32},{20,36},{24,40},{28,44},{32,4... | collective-permute-start | bytes 98312 | tf_op jit(solution)/shard_map/ppermute | solution.py:12
  168.5 7.6 %collective-permute-start.21 = (bf16[2,2,16,256]{3,2,1,0:T(8,128)(2,1)S(1)}, bf16[2,2,16,256]{3,2,1,0:T(8,128)(2,1)S(1)}, u32[]{:S(2)}, u32[]{:S(2)}) collective-permute-start(bf16[2,2,16,256]{3,2,1,0:T(8,128)(2,1)S(1)} %broadcast_select_fusion.16), channel_id=1, source_target_pairs={{0,32},{4,36},{8,40},{12,44},{16,48},{20,52},{24,56},{28,60},{32,6... | collective-permute-start | bytes 98312 | tf_op jit(solution)/shard_map/ppermute | solution.py:12
  170.1 11.8 %collective-permute-start.15 = (bf16[2,2,16,256]{3,2,1,0:T(8,128)(2,1)S(1)}, bf16[2,2,16,256]{3,2,1,0:T(8,128)(2,1)S(1)}, u32[]{:S(2)}, u32[]{:S(2)}) collective-permute-start(bf16[2,2,16,256]{3,2,1,0:T(8,128)(2,1)S(1)} %broadcast_select_fusion.21), channel_id=1, source_target_pairs={{0,32},{4,36},{8,40},{12,44},{16,48},{20,52},{24,56},{28,60},{32,6... | collective-permute-start | bytes 98312 | tf_op jit(solution)/shard_map/ppermute | solution.py:12
  170.2 18.9 %collective-permute-start.8 = (bf16[16,2048]{1,0:T(8,128)(2,1)S(1)}, bf16[16,2048]{1,0:T(8,128)(2,1)S(1)}, u32[]{:S(2)}, u32[]{:S(2)}) collective-permute-start(bf16[16,2048]{1,0:T(8,128)(2,1)S(1)} %broadcast_select_fusion.3), channel_id=1, source_target_pairs={{0,16},{4,20},{8,24},{12,28},{16,32},{20,36},{24,40},{28,44},{32,4... | collective-permute-start | bytes 196616 | tf_op jit(solution)/shard_map/ppermute | solution.py:12
  173.6 16.1 %collective-permute-start.2 = (bf16[16,2048]{1,0:T(8,128)(2,1)S(1)}, bf16[16,2048]{1,0:T(8,128)(2,1)S(1)}, u32[]{:S(2)}, u32[]{:S(2)}) collective-permute-start(bf16[16,2048]{1,0:T(8,128)(2,1)S(1)} %broadcast_select_fusion.9), channel_id=1, source_target_pairs={{0,16},{4,20},{8,24},{12,28},{16,32},{20,36},{24,40},{28,44},{32,4... | collective-permute-start | bytes 196616 | tf_op jit(solution)/shard_map/ppermute | solution.py:12
  176.1 7.9 %collective-permute-start.22 = (bf16[2,2,16,256]{3,2,1,0:T(8,128)(2,1)S(1)}, bf16[2,2,16,256]{3,2,1,0:T(8,128)(2,1)S(1)}, u32[]{:S(2)}, u32[]{:S(2)}) collective-permute-start(bf16[2,2,16,256]{3,2,1,0:T(8,128)(2,1)S(1)} %broadcast_select_fusion.17), channel_id=1, source_target_pairs={{0,64},{4,68},{8,72},{12,76},{16,80},{20,84},{24,88},{28,92},{32,9... | collective-permute-start | bytes 98312 | tf_op jit(solution)/shard_map/ppermute | solution.py:12
  181.9 7.1 %collective-permute-start.16 = (bf16[2,2,16,256]{3,2,1,0:T(8,128)(2,1)S(1)}, bf16[2,2,16,256]{3,2,1,0:T(8,128)(2,1)S(1)}, u32[]{:S(2)}, u32[]{:S(2)}) collective-permute-start(bf16[2,2,16,256]{3,2,1,0:T(8,128)(2,1)S(1)} %broadcast_select_fusion.22), channel_id=1, source_target_pairs={{0,64},{4,68},{8,72},{12,76},{16,80},{20,84},{24,88},{28,92},{32,9... | collective-permute-start | bytes 98312 | tf_op jit(solution)/shard_map/ppermute | solution.py:12
  184.0 5.8 %collective-permute-start.23 = (bf16[2,2,16,256]{3,2,1,0:T(8,128)(2,1)S(1)}, bf16[2,2,16,256]{3,2,1,0:T(8,128)(2,1)S(1)}, u32[]{:S(2)}, u32[]{:S(2)}) collective-permute-start(bf16[2,2,16,256]{3,2,1,0:T(8,128)(2,1)S(1)} %broadcast_select_fusion.18), channel_id=1, source_target_pairs={{0,128},{4,132},{8,136},{12,140},{16,144},{20,148},{24,152},{28,15... | collective-permute-start | bytes 98312 | tf_op jit(solution)/shard_map/ppermute | solution.py:12
  189.0 29.7 %collective-permute-start.17 = (bf16[2,2,16,256]{3,2,1,0:T(8,128)(2,1)S(1)}, bf16[2,2,16,256]{3,2,1,0:T(8,128)(2,1)S(1)}, u32[]{:S(2)}, u32[]{:S(2)}) collective-permute-start(bf16[2,2,16,256]{3,2,1,0:T(8,128)(2,1)S(1)} %broadcast_select_fusion.23), channel_id=1, source_target_pairs={{0,128},{4,132},{8,136},{12,140},{16,144},{20,148},{24,152},{28,15... | collective-permute-start | bytes 98312 | tf_op jit(solution)/shard_map/ppermute | solution.py:12
  189.2 31.7 %collective-permute-start.9 = (bf16[16,2048]{1,0:T(8,128)(2,1)S(1)}, bf16[16,2048]{1,0:T(8,128)(2,1)S(1)}, u32[]{:S(2)}, u32[]{:S(2)}) collective-permute-start(bf16[16,2048]{1,0:T(8,128)(2,1)S(1)} %broadcast_select_fusion.4), channel_id=1, source_target_pairs={{0,32},{4,36},{8,40},{12,44},{16,48},{20,52},{24,56},{28,60},{32,6... | collective-permute-start | bytes 196616 | tf_op jit(solution)/shard_map/ppermute | solution.py:12
  189.7 34.3 %collective-permute-start.3 = (bf16[16,2048]{1,0:T(8,128)(2,1)S(1)}, bf16[16,2048]{1,0:T(8,128)(2,1)S(1)}, u32[]{:S(2)}, u32[]{:S(2)}) collective-permute-start(bf16[16,2048]{1,0:T(8,128)(2,1)S(1)} %broadcast_select_fusion.10), channel_id=1, source_target_pairs={{0,32},{4,36},{8,40},{12,44},{16,48},{20,52},{24,56},{28,60},{32,6... | collective-permute-start | bytes 196616 | tf_op jit(solution)/shard_map/ppermute | solution.py:12
  197.0 73.5 %all-to-all-start.1 = ((f32[64,2,4096]{2,1,0:T(2,128)}), f32[64,2,4096]{2,1,0:T(2,128)}, u32[]{:S(2)}, u32[]{:S(2)}) async-start(f32[64,2,4096]{2,1,0:T(2,128)} %reshape.264), calls=%async_computation.2 | async-start | bytes 4194304 | tf_op jit(solution)/shard_map/all_to_all | solution.py:117
  218.6 19.7 %copy-start.1 = (bf16[16,16,2048]{2,1,0:T(8,128)(2,1)S(1)}, bf16[16,16,2048]{2,1,0:T(8,128)(2,1)}, u32[]{:S(2)}) copy-start(bf16[16,16,2048]{2,1,0:T(8,128)(2,1)} %param.17) | copy-start | bytes 3145732
  220.9 7.1 %collective-permute-start.10 = (bf16[16,2048]{1,0:T(8,128)(2,1)S(1)}, bf16[16,2048]{1,0:T(8,128)(2,1)S(1)}, u32[]{:S(2)}, u32[]{:S(2)}) collective-permute-start(bf16[16,2048]{1,0:T(8,128)(2,1)S(1)} %broadcast_select_fusion.5), channel_id=1, source_target_pairs={{0,64},{4,68},{8,72},{12,76},{16,80},{20,84},{24,88},{28,92},{32,9... | collective-permute-start | bytes 196616 | tf_op jit(solution)/shard_map/ppermute | solution.py:12
  224.0 9.6 %collective-permute-start.4 = (bf16[16,2048]{1,0:T(8,128)(2,1)S(1)}, bf16[16,2048]{1,0:T(8,128)(2,1)S(1)}, u32[]{:S(2)}, u32[]{:S(2)}) collective-permute-start(bf16[16,2048]{1,0:T(8,128)(2,1)S(1)} %broadcast_select_fusion.11), channel_id=1, source_target_pairs={{0,64},{4,68},{8,72},{12,76},{16,80},{20,84},{24,88},{28,92},{32,9... | collective-permute-start | bytes 196616 | tf_op jit(solution)/shard_map/ppermute | solution.py:12
  228.0 5.8 %collective-permute-start.11 = (bf16[16,2048]{1,0:T(8,128)(2,1)S(1)}, bf16[16,2048]{1,0:T(8,128)(2,1)S(1)}, u32[]{:S(2)}, u32[]{:S(2)}) collective-permute-start(bf16[16,2048]{1,0:T(8,128)(2,1)S(1)} %broadcast_select_fusion.6), channel_id=1, source_target_pairs={{0,128},{4,132},{8,136},{12,140},{16,144},{20,148},{24,152},{28,15... | collective-permute-start | bytes 196616 | tf_op jit(solution)/shard_map/ppermute | solution.py:12
  233.7 4.6 %collective-permute-start.5 = (bf16[16,2048]{1,0:T(8,128)(2,1)S(1)}, bf16[16,2048]{1,0:T(8,128)(2,1)S(1)}, u32[]{:S(2)}, u32[]{:S(2)}) collective-permute-start(bf16[16,2048]{1,0:T(8,128)(2,1)S(1)} %broadcast_select_fusion.12), channel_id=1, source_target_pairs={{0,128},{4,132},{8,136},{12,140},{16,144},{20,148},{24,152},{28,15... | collective-permute-start | bytes 196616 | tf_op jit(solution)/shard_map/ppermute | solution.py:12
Sparse Core Ops, SparseCore 0:
  55.6 36.0 all-gather.1
  109.2 84.2 reduce-scatter.1
where the time goes:
time: 284 us; the launch traced here: 283 us
  waiting for transfers between devices  93.3 us (33%)
  starting transfers between devices  63.9 us (22%)
  blocking collectives  42.1 us (15%)
  between operations  25.4 us (9%)
  local copies, waits for them, and re-layouts  21.9 us (8%)
  matrix products  18.5 us (7%)
  other arithmetic  17.9 us (6%)
    ppermute x24, starting transfers between devices, passed_along(): return lax.ppermute(value, axis, pairs)  42.2 us
    all_to_all x1, blocking collectives, local(): lax.all_to_all(outgoing, 'dp', split_axis=0, concat_axis=0, tiled=True)  42.1 us
    all_gather x1, waiting for transfers between devices, local(): piece = lax.all_gather(rows_in, 'ep', axis=0, tiled=True)  36.1 us
    all_to_all x1, waiting for transfers between devices, local(): lax.all_to_all(summed.reshape(ranks, CAP, width), 'dp', split_axis=0, con...  30.9 us
    ppermute x24, waiting for transfers between devices, passed_along(): return lax.ppermute(value, axis, pairs)  22.6 us
    all_to_all x1, starting transfers between devices, local(): lax.all_to_all(summed.reshape(ranks, CAP, width), 'dp', split_axis=0, con...  21.6 us
    dot_general x1, matrix products, local(): jnp.dot(hidden, w_down[0], preferred_element_type=jnp.float32)  11 us
    dot_general x1, matrix products, local(): gate = jnp.dot(piece, w_gate[0], preferred_element_type=jnp.float32)  6.37 us
  transfers between devices with their start and end apart: 27, of which 11 were waited for; matrix products, arithmetic and copies ran while one was open for 10% of the time, Pallas kernels for 0%

commit v1 on v0

--- a/solution.py
+++ b/solution.py
@@ -104,7 +104,9 @@
     outgoing = jnp.repeat(packed.reshape(experts, CAP, width), group, axis=0)
     incoming = lax.all_to_all(outgoing, "dp", split_axis=0, concat_axis=0, tiled=True)
     rows_in = incoming.reshape(ranks * CAP, width)
-    piece = lax.all_gather(rows_in, "ep", axis=0, tiled=True)
+    piece = jnp.concatenate(
+        lax.all_to_all(jnp.stack([rows_in] * lax.axis_size("ep")), "ep", 0, 0), axis=0
+    )
     gate = jnp.dot(piece, w_gate[0], preferred_element_type=jnp.float32)
     upper = jnp.dot(piece, w_up[0], preferred_element_type=jnp.float32)
     hidden = (jax.nn.silu(gate) * upper).astype(jnp.bfloat16)

time: 284 us -> 296 us (1.042)
  blocking collectives: 42.1 us -> 95.2 us
  waiting for transfers between devices: 93.3 us -> 58.2 us
  starting transfers between devices: 63.9 us -> 56.4 us
  local copies, waits for them, and re-layouts: 21.9 us -> 25.7 us
  matrix products: 18.5 us -> 15.4 us
    all_to_all x0 -> x1, blocking collectives: none -> 53.1 us  [local(): lax.all_to_all(jnp.stack([rows_in] * lax.axis_size('ep')), 'ep', 0, 0)]
    all_gather x1 -> x0, waiting for transfers between devices: 36.1 us -> none  [local(): piece = lax.all_gather(rows_in, 'ep', axis=0, tiled=True)]
    ppermute x24, starting transfers between devices: 42.2 us -> 35.8 us  [passed_along(): return lax.ppermute(value, axis, pairs)]
    ppermute x24, waiting for transfers between devices: 22.6 us -> 27.3 us  [passed_along(): return lax.ppermute(value, axis, pairs)]
    another operation x0 -> x2, local copies, waits for them, and re-layouts: none -> 3.96 us  [local(): jnp.stack([rows_in] * lax.axis_size('ep'))]
    reduce_scatter x1, waiting for transfers between devices: 3.7 us -> 0.02 us  [local(): lax.psum_scatter(jnp.dot(hidden, w_down[0], preferred_element_type=jnp.fl...]
    dot_general x1, matrix products: 6.37 us -> 3.21 us  [local(): gate = jnp.dot(piece, w_gate[0], preferred_element_type=jnp.float32)]
  transfers between devices with their start and end apart: 27 -> 26, of which waited for: 11 -> 9; matrix products, arithmetic and copies ran while one was open for 10% -> 10% of each run, Pallas kernels for 0% -> 0%
where the time goes in v1:
time: 296 us; the launch traced here: 295 us
  blocking collectives  95.2 us (32%)
  waiting for transfers between devices  58.2 us (20%)
  starting transfers between devices  56.4 us (19%)
  between operations  25.9 us (9%)
  local copies, waits for them, and re-layouts  25.7 us (9%)
  other arithmetic  18 us (6%)
  matrix products  15.4 us (5%)
    all_to_all x1, blocking collectives, local(): lax.all_to_all(jnp.stack([rows_in] * lax.axis_size('ep')), 'ep', 0, 0)  53.1 us
    all_to_all x1, blocking collectives, local(): lax.all_to_all(outgoing, 'dp', split_axis=0, concat_axis=0, tiled=True)  42.1 us
    ppermute x24, starting transfers between devices, passed_along(): return lax.ppermute(value, axis, pairs)  35.8 us
    all_to_all x1, waiting for transfers between devices, local(): lax.all_to_all(summed.reshape(ranks, CAP, width), 'dp', split_axis=0, con...  30.9 us
    ppermute x24, waiting for transfers between devices, passed_along(): return lax.ppermute(value, axis, pairs)  27.3 us
    all_to_all x1, starting transfers between devices, local(): lax.all_to_all(summed.reshape(ranks, CAP, width), 'dp', split_axis=0, con...  20.5 us
    dot_general x1, matrix products, local(): jnp.dot(hidden, w_down[0], preferred_element_type=jnp.float32)  11 us
  transfers between devices with their start and end apart: 26, of which 9 were waited for; matrix products, arithmetic and copies ran while one was open for 10% of the time, Pallas kernels for 0%

profile of v1, /device:TPU:34, one launch (start us, length us, event | category | flops | bytes accessed | tf_op | source)
XLA Modules:
  0.0 294.7 jit_solution(11513694265407899246)
XLA Ops:
  7.2 0.9 broadcast_in_dim.175
  8.2 0.8 copy.30
  9.4 0.5 copy-done.7
  10.2 1.0 broadcast_in_dim.176
  11.2 42.1 %all_to_all.15 = bf16[64,2,4096]{2,1,0:T(2,128)(2,1)} all-to-all(bf16[64,2,4096]{2,1,0:T(2,128)(2,1)S(1)} %bitcast.104), channel_id=1, replica_groups=mesh['dp'=64,'ep'=4] {'dp'}, dimensions={0} | all-to-all | bytes 2097152 | tf_op jit(solution)/shard_map/all_to_all | solution.py:105
  53.3 2.2 stack_reshape.2
  55.5 1.7 stack.11
  57.3 53.1 %all_to_all.16 = bf16[4,128,4096]{2,1,0:T(8,128)(2,1)S(1)} all-to-all(bf16[4,128,4096]{2,1,0:T(8,128)(2,1)S(1)} %stack.11), channel_id=1, replica_groups=mesh['dp'=64,'ep'=4] {'ep'}, dimensions={0} | all-to-all | bytes 8388608 | tf_op jit(solution)/shard_map/all_to_all | solution.py:108
  110.4 2.0 copy-done.1
  112.4 3.2 %fusion.4 = f32[512,384]{1,0:T(8,128)} fusion(bf16[512,4096]{1,0:T(8,128)(2,1)S(1)} %bitcast.102, bf16[1,4096,384]{2,1,0:T(8,128)(2,1)S(1)} %copy-done.9), kind=kOutput, calls=%fused_computation.9 | convolution fusion | flops 1610612736 | bytes 8126464 | tf_op jit(solution)/shard_map/dot_general | solution.py:110
  115.6 11.0 %fusion = f32[512,4096]{1,0:T(8,128)} fusion(bf16[1,384,4096]{2,1,0:T(8,128)(2,1)S(1)} %copy-done, bf16[512,4096]{1,0:T(8,128)(2,1)} %bitcast.103, bf16[1,4096,384]{2,1,0:T(8,128)(2,1)} %param.15, f32[512,384]{1,0:T(8,128)} %fusion.4), kind=kOutput, calls=%fused_computation.5 | convolution fusion | flops 3222405120 | bytes 19660800 | tf_op jit(solution)/shard_map/dot_general | solution.py:114
  126.6 0.6 copy-done.4
  127.6 1.8 gather_fusion.1
  129.5 0.7 slice_bitcast_fusion.1
  130.2 1.0 collective-permute-start.6
  131.5 0.9 fusion.22
  132.4 1.6 gather_fusion.2
  134.3 0.6 slice_bitcast_fusion.3
  135.0 2.0 collective-permute-start.18
  137.1 0.6 fusion.29
  140.5 1.0 fusion.31
  141.5 0.7 gather_fusion.3
  143.5 0.7 constant_dynamic-slice_fusion.7
  144.1 0.6 constant_dynamic-slice_fusion.6
  144.8 0.7 fusion.30
  145.5 1.7 compare_and_fusion.1
  147.3 2.5 compare_and_fusion.5
  149.8 0.6 fusion.25
  150.4 0.7 fusion.28
  151.2 0.8 compare_reduce_fusion.1
  152.0 0.8 compare_reduce_fusion
  152.8 1.9 compare_and_fusion.3
  162.5 2.3 collective-permute-start.19
  164.8 3.1 %collective-permute-start.13 = (bf16[2,2,16,256]{3,2,1,0:T(8,128)(2,1)S(1)}, bf16[2,2,16,256]{3,2,1,0:T(8,128)(2,1)S(1)}, u32[]{:S(2)}, u32[]{:S(2)}) collective-permute-start(bf16[2,2,16,256]{3,2,1,0:T(8,128)(2,1)S(1)} %get-tuple-element.11), channel_id=1, source_target_pairs={{0,8},{4,12},{8,16},{12,20},{16,24},{20,28},{24,32},{28,36},{32,40... | collective-permute-start | bytes 98312 | tf_op jit(solution)/shard_map/ppermute | solution.py:12
  168.0 0.9 broadcast_select_fusion.8
  168.8 0.6 collective-permute-start.7
  169.4 1.1 collective-permute-start.1
  170.5 1.3 collective-permute-done.19
  171.8 2.9 collective-permute-start.20
  174.7 2.3 collective-permute-start.14
  177.0 5.8 %collective-permute-done.20 = bf16[2,2,16,256]{3,2,1,0:T(8,128)(2,1)S(1)} collective-permute-done((bf16[2,2,16,256]{3,2,1,0:T(8,128)(2,1)S(1)}, bf16[2,2,16,256]{3,2,1,0:T(8,128)(2,1)S(1)}, u32[]{:S(2)}, u32[]{:S(2)}) %collective-permute-start.20) | collective-permute-done | bytes 32800 | tf_op jit(solution)/shard_map/ppermute | solution.py:12
  182.9 3.0 %collective-permute-done.14 = bf16[2,2,16,256]{3,2,1,0:T(8,128)(2,1)S(1)} collective-permute-done((bf16[2,2,16,256]{3,2,1,0:T(8,128)(2,1)S(1)}, bf16[2,2,16,256]{3,2,1,0:T(8,128)(2,1)S(1)}, u32[]{:S(2)}, u32[]{:S(2)}) %collective-permute-start.14) | collective-permute-done | bytes 32800 | tf_op jit(solution)/shard_map/ppermute | solution.py:12
  186.0 1.5 collective-permute-start.8
  187.5 6.3 %collective-permute-start.2 = (bf16[16,2048]{1,0:T(8,128)(2,1)S(1)}, bf16[16,2048]{1,0:T(8,128)(2,1)S(1)}, u32[]{:S(2)}, u32[]{:S(2)}) collective-permute-start(bf16[16,2048]{1,0:T(8,128)(2,1)S(1)} %broadcast_select_fusion.9), channel_id=1, source_target_pairs={{0,16},{4,20},{8,24},{12,28},{16,32},{20,36},{24,40},{28,44},{32,4... | collective-permute-start | bytes 196616 | tf_op jit(solution)/shard_map/ppermute | solution.py:12
  193.9 4.5 %collective-permute-start.22 = (bf16[2,2,16,256]{3,2,1,0:T(8,128)(2,1)S(1)}, bf16[2,2,16,256]{3,2,1,0:T(8,128)(2,1)S(1)}, u32[]{:S(2)}, u32[]{:S(2)}) collective-permute-start(bf16[2,2,16,256]{3,2,1,0:T(8,128)(2,1)S(1)} %broadcast_select_fusion.17), channel_id=1, source_target_pairs={{0,64},{4,68},{8,72},{12,76},{16,80},{20,84},{24,88},{28,92},{32,9... | collective-permute-start | bytes 98312 | tf_op jit(solution)/shard_map/ppermute | solution.py:12
  198.5 2.8 collective-permute-done.22
  201.3 1.5 collective-permute-start.23
  202.8 2.6 collective-permute-done.16
  205.7 0.6 collective-permute-start.3
  206.3 3.5 %reshape.266 = f32[64,2,4096]{2,1,0:T(2,128)} reshape(f32[128,4096]{1,0:T(8,128)} %reduce-scatter.2.cloned.1.call-done) | data formatting | bytes 4194304 | tf_op jit(solution)/shard_map/reshape | solution.py:120
  209.8 20.5 %all-to-all-start.2 = ((f32[64,2,4096]{2,1,0:T(2,128)}), f32[64,2,4096]{2,1,0:T(2,128)}, u32[]{:S(2)}, u32[]{:S(2)}) async-start(f32[64,2,4096]{2,1,0:T(2,128)} %reshape.266), calls=%async_computation.3 | async-start | bytes 4194304 | tf_op jit(solution)/shard_map/all_to_all | solution.py:119
  230.4 2.2 select_select_fusion.1
  232.6 3.2 %collective-permute-start.10 = (bf16[16,2048]{1,0:T(8,128)(2,1)S(1)}, bf16[16,2048]{1,0:T(8,128)(2,1)S(1)}, u32[]{:S(2)}, u32[]{:S(2)}) collective-permute-start(bf16[16,2048]{1,0:T(8,128)(2,1)S(1)} %broadcast_select_fusion.5), channel_id=1, source_target_pairs={{0,64},{4,68},{8,72},{12,76},{16,80},{20,84},{24,88},{28,92},{32,9... | collective-permute-start | bytes 196616 | tf_op jit(solution)/shard_map/ppermute | solution.py:12
  235.8 0.4 collective-permute-start.4
  236.2 3.6 %collective-permute-done.10 = bf16[16,2048]{1,0:T(8,128)(2,1)S(1)} collective-permute-done((bf16[16,2048]{1,0:T(8,128)(2,1)S(1)}, bf16[16,2048]{1,0:T(8,128)(2,1)S(1)}, u32[]{:S(2)}, u32[]{:S(2)}) %collective-permute-start.10) | collective-permute-done | bytes 65568 | tf_op jit(solution)/shard_map/ppermute | solution.py:12
  239.8 1.9 collective-permute-start.11
  241.7 3.7 %collective-permute-done.4 = bf16[16,2048]{1,0:T(8,128)(2,1)S(1)} collective-permute-done((bf16[16,2048]{1,0:T(8,128)(2,1)S(1)}, bf16[16,2048]{1,0:T(8,128)(2,1)S(1)}, u32[]{:S(2)}, u32[]{:S(2)}) %collective-permute-start.4) | collective-permute-done | bytes 65568 | tf_op jit(solution)/shard_map/ppermute | solution.py:12
  245.5 4.5 %collective-permute-done.5 = bf16[16,2048]{1,0:T(8,128)(2,1)S(1)} collective-permute-done((bf16[16,2048]{1,0:T(8,128)(2,1)S(1)}, bf16[16,2048]{1,0:T(8,128)(2,1)S(1)}, u32[]{:S(2)}, u32[]{:S(2)}) %collective-permute-start.5) | collective-permute-done | bytes 65568 | tf_op jit(solution)/shard_map/ppermute | solution.py:12
  250.0 1.3 select_select_fusion
  251.3 30.9 %all-to-all-done.2 = f32[64,2,4096]{2,1,0:T(2,128)} async-done(((f32[64,2,4096]{2,1,0:T(2,128)}), f32[64,2,4096]{2,1,0:T(2,128)}, u32[]{:S(2)}, u32[]{:S(2)}) %all-to-all-start.2) | async-done | bytes 2097184 | tf_op jit(solution)/shard_map/all_to_all | solution.py:119
  282.2 3.0 %bitcast_reduce_fusion = f32[8,2,4096]{2,1,0:T(2,128)} fusion(f32[64,2,4096]{2,1,0:T(2,128)} %all-to-all-done.2), kind=kLoop, calls=%fused_computation.11 | loop fusion | flops 458752 | bytes 2359296 | tf_op jit(solution)/shard_map/reduce_sum | solution.py:122
  285.2 1.1 reshape.268
  286.3 0.6 gather_fusion
  287.0 0.9 multiply_reduce_fusion
  (103 shorter events, 3.6 us)
Async XLA Ops:
  7.2 108.4 %copy-start = (bf16[1,384,4096]{2,1,0:T(8,128)(2,1)S(1)}, bf16[1,384,4096]{2,1,0:T(8,128)(2,1)}, u32[]{:S(2)}) copy-start(bf16[1,384,4096]{2,1,0:T(8,128)(2,1)} %param.16) | copy-start | bytes 9437188
  7.2 199.1 %reduce-scatter.2.cloned.1.call-start = ((), (), s32[]{:S(2)}) async-start(), calls=%async_computation.4 | async-start | bytes 10485760 | tf_op jit(solution)/shard_map/reduce_scatter | solution.py:113
  9.3 0.5 copy-start.7
  57.3 55.1 %copy-start.9 = (bf16[1,4096,384]{2,1,0:T(8,128)(2,1)S(1)}, bf16[1,4096,384]{2,1,0:T(8,128)(2,1)}, u32[]{:S(2)}) copy-start(bf16[1,4096,384]{2,1,0:T(8,128)(2,1)} %param.14) | copy-start | bytes 9437188
  110.4 2.0 copy-start.1
  126.6 0.7 copy-start.4
  126.6 4.6 %copy-start.5 = (s32[64,2,2,2]{0,3,2,1:T(2,128)S(1)}, s32[64,2,2,2]{0,3,2,1:T(2,128)}, u32[]{:S(2)}) copy-start(s32[64,2,2,2]{0,3,2,1:T(2,128)} %param.21) | copy-start | bytes 6148
  126.6 13.9 %copy-start.3 = (f32[4096,8]{0,1:T(8,128)S(1)}, f32[4096,8]{0,1:T(8,128)}, u32[]{:S(2)}) copy-start(f32[4096,8]{0,1:T(8,128)} %param.12) | copy-start | bytes 393220
  127.6 1.8 copy-start.8
  130.2 37.8 %collective-permute-start = (bf16[16,2048]{1,0:T(8,128)(2,1)}, bf16[16,2048]{1,0:T(8,128)(2,1)}, u32[]{:S(2)}, u32[]{:S(2)}) collective-permute-start(bf16[16,2048]{1,0:T(8,128)(2,1)} %get-tuple-element.9), channel_id=1, source_target_pairs={{0,4},{4,8},{8,12},{12,16},{16,20},{20,24},{24,28},{28,32},{32,36}... | collective-permute-start | bytes 196616 | tf_op jit(solution)/shard_map/ppermute | solution.py:12
  130.2 37.8 %collective-permute-start.6 = (bf16[16,2048]{1,0:T(8,128)(2,1)}, bf16[16,2048]{1,0:T(8,128)(2,1)}, u32[]{:S(2)}, u32[]{:S(2)}) collective-permute-start(bf16[16,2048]{1,0:T(8,128)(2,1)} %get-tuple-element.10), channel_id=1, source_target_pairs={{0,4},{4,8},{8,12},{12,16},{16,20},{20,24},{24,28},{28,32},{32,36}... | collective-permute-start | bytes 196616 | tf_op jit(solution)/shard_map/ppermute | solution.py:12
  131.4 2.8 copy-start.6
  134.9 27.6 %collective-permute-start.12 = (bf16[2,2,16,256]{3,2,1,0:T(8,128)(2,1)}, bf16[2,2,16,256]{3,2,1,0:T(8,128)(2,1)S(1)}, u32[]{:S(2)}, u32[]{:S(2)}) collective-permute-start(bf16[2,2,16,256]{3,2,1,0:T(8,128)(2,1)} %get-tuple-element.13), channel_id=1, source_target_pairs={{0,4},{4,8},{8,12},{12,16},{16,20},{20,24},{24,28},{28,32},{32,36}... | collective-permute-start | bytes 98312 | tf_op jit(solution)/shard_map/ppermute | solution.py:12
  135.0 27.5 %collective-permute-start.18 = (bf16[2,2,16,256]{3,2,1,0:T(8,128)(2,1)}, bf16[2,2,16,256]{3,2,1,0:T(8,128)(2,1)}, u32[]{:S(2)}, u32[]{:S(2)}) collective-permute-start(bf16[2,2,16,256]{3,2,1,0:T(8,128)(2,1)} %get-tuple-element.14), channel_id=1, source_target_pairs={{0,4},{4,8},{8,12},{12,16},{16,20},{20,24},{24,28},{28,32},{32,36}... | collective-permute-start | bytes 98312 | tf_op jit(solution)/shard_map/ppermute | solution.py:12
  162.5 9.3 %collective-permute-start.19 = (bf16[2,2,16,256]{3,2,1,0:T(8,128)(2,1)S(1)}, bf16[2,2,16,256]{3,2,1,0:T(8,128)(2,1)S(1)}, u32[]{:S(2)}, u32[]{:S(2)}) collective-permute-start(bf16[2,2,16,256]{3,2,1,0:T(8,128)(2,1)S(1)} %get-tuple-element.12), channel_id=1, source_target_pairs={{0,8},{4,12},{8,16},{12,20},{16,24},{20,28},{24,32},{28,36},{32,40... | collective-permute-start | bytes 98312 | tf_op jit(solution)/shard_map/ppermute | solution.py:12
  164.8 9.9 %collective-permute-start.13 = (bf16[2,2,16,256]{3,2,1,0:T(8,128)(2,1)S(1)}, bf16[2,2,16,256]{3,2,1,0:T(8,128)(2,1)S(1)}, u32[]{:S(2)}, u32[]{:S(2)}) collective-permute-start(bf16[2,2,16,256]{3,2,1,0:T(8,128)(2,1)S(1)} %get-tuple-element.11), channel_id=1, source_target_pairs={{0,8},{4,12},{8,16},{12,20},{16,24},{20,28},{24,32},{28,36},{32,40... | collective-permute-start | bytes 98312 | tf_op jit(solution)/shard_map/ppermute | solution.py:12
  168.8 17.2 %collective-permute-start.7 = (bf16[16,2048]{1,0:T(8,128)(2,1)S(1)}, bf16[16,2048]{1,0:T(8,128)(2,1)S(1)}, u32[]{:S(2)}, u32[]{:S(2)}) collective-permute-start(bf16[16,2048]{1,0:T(8,128)(2,1)S(1)} %get-tuple-element.8), channel_id=1, source_target_pairs={{0,8},{4,12},{8,16},{12,20},{16,24},{20,28},{24,32},{28,36},{32,40... | collective-permute-start | bytes 196616 | tf_op jit(solution)/shard_map/ppermute | solution.py:12
  169.4 18.1 %collective-permute-start.1 = (bf16[16,2048]{1,0:T(8,128)(2,1)S(1)}, bf16[16,2048]{1,0:T(8,128)(2,1)S(1)}, u32[]{:S(2)}, u32[]{:S(2)}) collective-permute-start(bf16[16,2048]{1,0:T(8,128)(2,1)S(1)} %get-tuple-element.7), channel_id=1, source_target_pairs={{0,8},{4,12},{8,16},{12,20},{16,24},{20,28},{24,32},{28,36},{32,40... | collective-permute-start | bytes 196616 | tf_op jit(solution)/shard_map/ppermute | solution.py:12
  171.8 11.0 %collective-permute-start.20 = (bf16[2,2,16,256]{3,2,1,0:T(8,128)(2,1)S(1)}, bf16[2,2,16,256]{3,2,1,0:T(8,128)(2,1)S(1)}, u32[]{:S(2)}, u32[]{:S(2)}) collective-permute-start(bf16[2,2,16,256]{3,2,1,0:T(8,128)(2,1)S(1)} %broadcast_select_fusion.15), channel_id=1, source_target_pairs={{0,16},{4,20},{8,24},{12,28},{16,32},{20,36},{24,40},{28,44},{32,4... | collective-permute-start | bytes 98312 | tf_op jit(solution)/shard_map/ppermute | solution.py:12
  174.7 11.2 %collective-permute-start.14 = (bf16[2,2,16,256]{3,2,1,0:T(8,128)(2,1)S(1)}, bf16[2,2,16,256]{3,2,1,0:T(8,128)(2,1)S(1)}, u32[]{:S(2)}, u32[]{:S(2)}) collective-permute-start(bf16[2,2,16,256]{3,2,1,0:T(8,128)(2,1)S(1)} %broadcast_select_fusion.20), channel_id=1, source_target_pairs={{0,16},{4,20},{8,24},{12,28},{16,32},{20,36},{24,40},{28,44},{32,4... | collective-permute-start | bytes 98312 | tf_op jit(solution)/shard_map/ppermute | solution.py:12
  182.8 11.1 %collective-permute-start.21 = (bf16[2,2,16,256]{3,2,1,0:T(8,128)(2,1)S(1)}, bf16[2,2,16,256]{3,2,1,0:T(8,128)(2,1)S(1)}, u32[]{:S(2)}, u32[]{:S(2)}) collective-permute-start(bf16[2,2,16,256]{3,2,1,0:T(8,128)(2,1)S(1)} %broadcast_select_fusion.16), channel_id=1, source_target_pairs={{0,32},{4,36},{8,40},{12,44},{16,48},{20,52},{24,56},{28,60},{32,6... | collective-permute-start | bytes 98312 | tf_op jit(solution)/shard_map/ppermute | solution.py:12
  185.9 12.5 %collective-permute-start.15 = (bf16[2,2,16,256]{3,2,1,0:T(8,128)(2,1)S(1)}, bf16[2,2,16,256]{3,2,1,0:T(8,128)(2,1)S(1)}, u32[]{:S(2)}, u32[]{:S(2)}) collective-permute-start(bf16[2,2,16,256]{3,2,1,0:T(8,128)(2,1)S(1)} %broadcast_select_fusion.21), channel_id=1, source_target_pairs={{0,32},{4,36},{8,40},{12,44},{16,48},{20,52},{24,56},{28,60},{32,6... | collective-permute-start | bytes 98312 | tf_op jit(solution)/shard_map/ppermute | solution.py:12
  186.0 19.5 %collective-permute-start.8 = (bf16[16,2048]{1,0:T(8,128)(2,1)S(1)}, bf16[16,2048]{1,0:T(8,128)(2,1)S(1)}, u32[]{:S(2)}, u32[]{:S(2)}) collective-permute-start(bf16[16,2048]{1,0:T(8,128)(2,1)S(1)} %broadcast_select_fusion.3), channel_id=1, source_target_pairs={{0,16},{4,20},{8,24},{12,28},{16,32},{20,36},{24,40},{28,44},{32,4... | collective-permute-start | bytes 196616 | tf_op jit(solution)/shard_map/ppermute | solution.py:12
  187.5 18.1 %collective-permute-start.2 = (bf16[16,2048]{1,0:T(8,128)(2,1)S(1)}, bf16[16,2048]{1,0:T(8,128)(2,1)S(1)}, u32[]{:S(2)}, u32[]{:S(2)}) collective-permute-start(bf16[16,2048]{1,0:T(8,128)(2,1)S(1)} %broadcast_select_fusion.9), channel_id=1, source_target_pairs={{0,16},{4,20},{8,24},{12,28},{16,32},{20,36},{24,40},{28,44},{32,4... | collective-permute-start | bytes 196616 | tf_op jit(solution)/shard_map/ppermute | solution.py:12
  193.9 7.4 %collective-permute-start.22 = (bf16[2,2,16,256]{3,2,1,0:T(8,128)(2,1)S(1)}, bf16[2,2,16,256]{3,2,1,0:T(8,128)(2,1)S(1)}, u32[]{:S(2)}, u32[]{:S(2)}) collective-permute-start(bf16[2,2,16,256]{3,2,1,0:T(8,128)(2,1)S(1)} %broadcast_select_fusion.17), channel_id=1, source_target_pairs={{0,64},{4,68},{8,72},{12,76},{16,80},{20,84},{24,88},{28,92},{32,9... | collective-permute-start | bytes 98312 | tf_op jit(solution)/shard_map/ppermute | solution.py:12
  198.4 7.0 %collective-permute-start.16 = (bf16[2,2,16,256]{3,2,1,0:T(8,128)(2,1)S(1)}, bf16[2,2,16,256]{3,2,1,0:T(8,128)(2,1)S(1)}, u32[]{:S(2)}, u32[]{:S(2)}) collective-permute-start(bf16[2,2,16,256]{3,2,1,0:T(8,128)(2,1)S(1)} %broadcast_select_fusion.22), channel_id=1, source_target_pairs={{0,64},{4,68},{8,72},{12,76},{16,80},{20,84},{24,88},{28,92},{32,9... | collective-permute-start | bytes 98312 | tf_op jit(solution)/shard_map/ppermute | solution.py:12
  201.3 5.0 %collective-permute-start.23 = (bf16[2,2,16,256]{3,2,1,0:T(8,128)(2,1)S(1)}, bf16[2,2,16,256]{3,2,1,0:T(8,128)(2,1)S(1)}, u32[]{:S(2)}, u32[]{:S(2)}) collective-permute-start(bf16[2,2,16,256]{3,2,1,0:T(8,128)(2,1)S(1)} %broadcast_select_fusion.18), channel_id=1, source_target_pairs={{0,128},{4,132},{8,136},{12,140},{16,144},{20,148},{24,152},{28,15... | collective-permute-start | bytes 98312 | tf_op jit(solution)/shard_map/ppermute | solution.py:12
  205.5 24.9 %collective-permute-start.17 = (bf16[2,2,16,256]{3,2,1,0:T(8,128)(2,1)S(1)}, bf16[2,2,16,256]{3,2,1,0:T(8,128)(2,1)S(1)}, u32[]{:S(2)}, u32[]{:S(2)}) collective-permute-start(bf16[2,2,16,256]{3,2,1,0:T(8,128)(2,1)S(1)} %broadcast_select_fusion.23), channel_id=1, source_target_pairs={{0,128},{4,132},{8,136},{12,140},{16,144},{20,148},{24,152},{28,15... | collective-permute-start | bytes 98312 | tf_op jit(solution)/shard_map/ppermute | solution.py:12
  205.6 27.0 %collective-permute-start.9 = (bf16[16,2048]{1,0:T(8,128)(2,1)S(1)}, bf16[16,2048]{1,0:T(8,128)(2,1)S(1)}, u32[]{:S(2)}, u32[]{:S(2)}) collective-permute-start(bf16[16,2048]{1,0:T(8,128)(2,1)S(1)} %broadcast_select_fusion.4), channel_id=1, source_target_pairs={{0,32},{4,36},{8,40},{12,44},{16,48},{20,52},{24,56},{28,60},{32,6... | collective-permute-start | bytes 196616 | tf_op jit(solution)/shard_map/ppermute | solution.py:12
  205.7 30.0 %collective-permute-start.3 = (bf16[16,2048]{1,0:T(8,128)(2,1)S(1)}, bf16[16,2048]{1,0:T(8,128)(2,1)S(1)}, u32[]{:S(2)}, u32[]{:S(2)}) collective-permute-start(bf16[16,2048]{1,0:T(8,128)(2,1)S(1)} %broadcast_select_fusion.10), channel_id=1, source_target_pairs={{0,32},{4,36},{8,40},{12,44},{16,48},{20,52},{24,56},{28,60},{32,6... | collective-permute-start | bytes 196616 | tf_op jit(solution)/shard_map/ppermute | solution.py:12
  209.8 72.4 %all-to-all-start.2 = ((f32[64,2,4096]{2,1,0:T(2,128)}), f32[64,2,4096]{2,1,0:T(2,128)}, u32[]{:S(2)}, u32[]{:S(2)}) async-start(f32[64,2,4096]{2,1,0:T(2,128)} %reshape.266), calls=%async_computation.3 | async-start | bytes 4194304 | tf_op jit(solution)/shard_map/all_to_all | solution.py:119
  230.3 19.7 %copy-start.2 = (bf16[16,16,2048]{2,1,0:T(8,128)(2,1)S(1)}, bf16[16,16,2048]{2,1,0:T(8,128)(2,1)}, u32[]{:S(2)}) copy-start(bf16[16,16,2048]{2,1,0:T(8,128)(2,1)} %param.17) | copy-start | bytes 3145732
  232.6 7.2 %collective-permute-start.10 = (bf16[16,2048]{1,0:T(8,128)(2,1)S(1)}, bf16[16,2048]{1,0:T(8,128)(2,1)S(1)}, u32[]{:S(2)}, u32[]{:S(2)}) collective-permute-start(bf16[16,2048]{1,0:T(8,128)(2,1)S(1)} %broadcast_select_fusion.5), channel_id=1, source_target_pairs={{0,64},{4,68},{8,72},{12,76},{16,80},{20,84},{24,88},{28,92},{32,9... | collective-permute-start | bytes 196616 | tf_op jit(solution)/shard_map/ppermute | solution.py:12
  235.8 9.6 %collective-permute-start.4 = (bf16[16,2048]{1,0:T(8,128)(2,1)S(1)}, bf16[16,2048]{1,0:T(8,128)(2,1)S(1)}, u32[]{:S(2)}, u32[]{:S(2)}) collective-permute-start(bf16[16,2048]{1,0:T(8,128)(2,1)S(1)} %broadcast_select_fusion.11), channel_id=1, source_target_pairs={{0,64},{4,68},{8,72},{12,76},{16,80},{20,84},{24,88},{28,92},{32,9... | collective-permute-start | bytes 196616 | tf_op jit(solution)/shard_map/ppermute | solution.py:12
  239.8 5.7 %collective-permute-start.11 = (bf16[16,2048]{1,0:T(8,128)(2,1)S(1)}, bf16[16,2048]{1,0:T(8,128)(2,1)S(1)}, u32[]{:S(2)}, u32[]{:S(2)}) collective-permute-start(bf16[16,2048]{1,0:T(8,128)(2,1)S(1)} %broadcast_select_fusion.6), channel_id=1, source_target_pairs={{0,128},{4,132},{8,136},{12,140},{16,144},{20,148},{24,152},{28,15... | collective-permute-start | bytes 196616 | tf_op jit(solution)/shard_map/ppermute | solution.py:12
  245.4 4.6 %collective-permute-start.5 = (bf16[16,2048]{1,0:T(8,128)(2,1)S(1)}, bf16[16,2048]{1,0:T(8,128)(2,1)S(1)}, u32[]{:S(2)}, u32[]{:S(2)}) collective-permute-start(bf16[16,2048]{1,0:T(8,128)(2,1)S(1)} %broadcast_select_fusion.12), channel_id=1, source_target_pairs={{0,128},{4,132},{8,136},{12,140},{16,144},{20,148},{24,152},{28,15... | collective-permute-start | bytes 196616 | tf_op jit(solution)/shard_map/ppermute | solution.py:12
Sparse Core Ops, SparseCore 0:
  126.8 77.8 reduce-scatter.1
